TPU v7x, 32 devices: a whole 2x2x4 slice. The times are simulated.
32 devices in a mesh: wide: 8 (over z, core), narrow: 4 (over y, x).
Axes of the slice: x: 2, y: 2, z: 4, core: 2. Of those that a mesh axis runs over, the one named last changes fastest.
Arguments:
- homolog_embedding: float32 [32, 1024, 256], P('wide', 'narrow'), may hold values from -6 to 6
- pair_state: float32 [1024, 1024, 128], P('wide', 'narrow'), may hold values from -6 to 6
- probe_projector: float32 [256, 256], replicated, may hold values from -0.375 to 0.375
- lookup_projector: float32 [256, 256], replicated, may hold values from -0.375 to 0.375
- content_projector: float32 [256, 256], replicated, may hold values from -0.375 to 0.375
- sigmoid_projector: float32 [256, 256], replicated, may hold values from -0.375 to 0.375
- sigmoid_offset: float32 [256], replicated, may hold values from -4 to 4
- pair_bias_weight: float32 [128, 8], replicated, may hold values from -4 to 4
- mixing_projector: float32 [256, 256], replicated, may hold values from -0.375 to 0.375
- mixing_offset: float32 [256], replicated, may hold values from -3 to 3
- first_factor_projector: float32 [256, 32], replicated, may hold values from -0.375 to 0.375
- second_factor_projector: float32 [256, 32], replicated, may hold values from -0.375 to 0.375
- outer_product_weight: float32 [1024, 128], replicated, may hold values from -0.5 to 0.5
- outer_product_bias: float32 [128], replicated, may hold values from -3 to 3
- up_weight: float32 [128, 512], replicated, may hold values from -0.5 to 0.5
- expand_bias: float32 [512], replicated, may hold values from -3 to 3
- down_weight: float32 [512, 128], replicated, may hold values from -0.25 to 0.25
Outputs:
- alignment_state_next: float32 [32, 1024, 256], P('wide', 'narrow')
- pair_state_next: float32 [1024, 1024, 128], P('wide', 'narrow')
All inputs are finite; a program needn't handle non-finite values.
Results may differ from a plain program's by a relative error of at most 0.0003.
Values sent between devices are 32-bit elements; how exact they have to be, the bound alone decides.
No kernel may reach another device: no remote copies, remote signals or barrier semaphores. Data moves between devices by JAX's collectives and lax.ppermute only.
A program may use at most 192 MiB of HBM per device.

v0:
```python
import math
import jax
import jax.numpy as jnp
from jax import lax
from jax.sharding import PartitionSpec as P

finest_precision = lax.Precision.HIGHEST


def layer_normalize(tensor):
    row_mean = jnp.mean(tensor, axis=-1, keepdims=True)
    centered = tensor - row_mean
    variance = jnp.mean(centered * centered, axis=-1, keepdims=True)
    return centered * lax.rsqrt(variance + 1e-05)


def matrix_multiply(first_arr, second_arr):
    return jnp.dot(
        first_arr, second_arr, precision=finest_precision, preferred_element_type=jnp.float32
    )


def per_device(
    homolog_embedding,
    pair_state,
    probe_projector,
    lookup_projector,
    content_projector,
    sigmoid_projector,
    sigmoid_offset,
    pair_bias_weight,
    mixing_projector,
    mixing_offset,
    first_factor_projector,
    second_factor_projector,
    outer_product_weight,
    outer_product_bias,
    up_weight,
    expand_bias,
    down_weight,
):
    head_count = pair_bias_weight.shape[1]
    channel_count = homolog_embedding.shape[2]
    head_width = channel_count // head_count
    alignment_normed = layer_normalize(homolog_embedding)
    query_vectors = matrix_multiply(alignment_normed, probe_projector) / math.sqrt(head_width)
    key_rows = matrix_multiply(alignment_normed, lookup_projector)
    value_rows = matrix_multiply(alignment_normed, content_projector)
    gate_logits = matrix_multiply(alignment_normed, sigmoid_projector) + sigmoid_offset
    bias_tile = jnp.einsum(
        "ijc,ch->hij", layer_normalize(pair_state), pair_bias_weight, precision=finest_precision
    )
    own_heads = lax.all_to_all(bias_tile, "narrow", split_axis=0, concat_axis=2, tiled=True)
    pair_bias = lax.all_gather(own_heads, "wide", axis=1, tiled=True)
    operands = (
        lax.all_to_all(query_vectors, "narrow", split_axis=2, concat_axis=1, tiled=True),
        lax.all_to_all(key_rows, "narrow", split_axis=2, concat_axis=1, tiled=True),
        lax.all_to_all(value_rows, "narrow", split_axis=2, concat_axis=1, tiled=True),
        lax.all_to_all(gate_logits, "narrow", split_axis=2, concat_axis=1, tiled=True),
    )
    seq_len = operands[0].shape[1]
    local_width = operands[0].shape[2]
    local_heads = pair_bias.shape[0]
    local_size = local_width // local_heads
    row_span = min(512, seq_len)
    span_count = seq_len // row_span

    def per_item(item_parts):
        query_item = item_parts[0].reshape(seq_len, local_heads, local_size)
        key_item = item_parts[1].reshape(seq_len, local_heads, local_size)
        value_item = item_parts[2].reshape(seq_len, local_heads, local_size)

        def per_block(block_index):
            query_rows = lax.dynamic_slice_in_dim(query_item, block_index * row_span, row_span, 0)
            bias_rows = lax.dynamic_slice_in_dim(pair_bias, block_index * row_span, row_span, 1)
            scores = (
                jnp.einsum("qhd,khd->hqk", query_rows, key_item, precision=finest_precision)
                + bias_rows
            )
            row_max = jnp.max(scores, axis=-1, keepdims=True)
            exponent = jnp.exp(scores - row_max)
            softmax_probabilities = exponent / jnp.sum(exponent, axis=-1, keepdims=True)
            returned_tensor = jnp.einsum(
                "hqk,khd->qhd", softmax_probabilities, value_item, precision=finest_precision
            )
            return returned_tensor.reshape(row_span, local_width)

        blocks = lax.map(per_block, jnp.arange(span_count, dtype=jnp.int32))
        return blocks.reshape(seq_len, local_width)

    outcome = lax.map(per_item, (operands[0], operands[1], operands[2]))
    outcome = outcome * jax.nn.sigmoid(operands[3])
    merged_heads = lax.all_to_all(outcome, "narrow", split_axis=1, concat_axis=2, tiled=True)
    alignment_state_next = (
        homolog_embedding + matrix_multiply(merged_heads, mixing_projector) + mixing_offset
    )
    outer_product_normed = layer_normalize(alignment_state_next)
    left_proj = jnp.einsum(
        "srm,mc->scr", outer_product_normed, first_factor_projector, precision=finest_precision
    )
    right_proj = jnp.einsum(
        "srm,mc->scr", outer_product_normed, second_factor_projector, precision=finest_precision
    )
    left_rows = lax.all_gather(left_proj, "narrow", axis=2, tiled=True)
    left_all = lax.all_to_all(left_rows, "wide", split_axis=2, concat_axis=0, tiled=True)
    seq_count = left_all.shape[0]
    tile_rows = left_all.shape[2]
    tile_cols = right_proj.shape[2]
    outer_width = left_all.shape[1] * right_proj.shape[1]
    right_all = lax.all_gather(right_proj, "wide", axis=0, tiled=True)
    block_rows = math.gcd(16, tile_rows)

    def outer_block(block_index):
        left_part = lax.dynamic_slice_in_dim(left_all, block_index * block_rows, block_rows, 2)
        product = (
            jnp.einsum("sci,sdj->ijcd", left_part, right_all, precision=finest_precision)
            / seq_count
        )
        flat = product.reshape(block_rows * tile_cols, outer_width)
        return matrix_multiply(flat, outer_product_weight).reshape(block_rows, tile_cols, -1)

    update = lax.map(outer_block, jnp.arange(tile_rows // block_rows, dtype=jnp.int32))
    update = update.reshape(tile_rows, tile_cols, -1)
    pair_mid = pair_state + update + outer_product_bias
    hidden = jax.nn.relu(matrix_multiply(layer_normalize(pair_mid), up_weight) + expand_bias)
    pair_state_next = pair_mid + matrix_multiply(hidden, down_weight)
    return (alignment_state_next, pair_state_next)


def solution(mesh):
    placed = (
        P("wide", "narrow", None),
        P("wide", "narrow", None),
        P(),
        P(),
        P(),
        P(),
        P(),
        P(),
        P(),
        P(),
        P(),
        P(),
        P(),
        P(),
        P(),
        P(),
        P(),
    )
    return jax.shard_map(
        per_device,
        mesh=mesh,
        in_specs=placed,
        out_specs=(P("wide", "narrow", None), P("wide", "narrow", None)),
        check_vma=False,
    )
```

profile of v0, /device:TPU:0, one launch (start us, length us, event | category | flops | bytes accessed | tf_op | source)
XLA Modules:
  0.0 893.6 jit_solution(2013924085573206081)
XLA Ops:
  26.8 27.4 %fusion.36 = f32[8,128,256]{2,0,1:T(8,128)S(1)} fusion(f32[128,256,128]{2,1,0:T(8,128)S(1)} %copy-done.1, f32[128,256]{1,0:T(8,128)S(1)} %add_rsqrt_fusion.1, f32[128,256]{1,0:T(8,128)S(1)} %broadcast_multiply_fusion.1, f32[128,8]{0,1:T(8,128)S(1)} %copy-done.11), kind=kOutput, calls=%fused_computation.49 | convolution fusion | flops 411041792 | bytes 18092032 | tf_op jit(solution)/shard_map/ijc,ch->hij/dot_general | solution.py:50
  54.6 19.1 %all_to_all.117 = f32[8,128,256]{2,1,0:T(8,128)S(1)} all-to-all(f32[8,128,256]{2,1,0:T(8,128)S(1)} %copy.112), channel_id=1, replica_groups=mesh['wide'=8,'narrow'=4] {'narrow'}, dimensions={0} | all-to-all | bytes 2097152 | tf_op jit(solution)/shard_map/all_to_all | solution.py:53
  156.8 111.2 %while.31 = (s32[]{:T(128)}, f32[4,1024,64]{1,2,0:T(8,128)}, f32[4,1024,64]{1,2,0:T(8,128)S(1)}, f32[4,1024,64]{1,2,0:T(8,128)}, f32[4,1024,64]{1,2,0:T(8,128)},...) while((s32[]{:T(128)}, f32[4,1024,64]{1,2,0:T(8,128)}, ...), condition=%wide.region_9.10_spmd, body=%wide.region_4.9_spmd.sunk | while | flops 811595776 | bytes 20993444 | solution.py:91
  157.9 25.5 %while.33 = (s32[]{:T(128)}, f32[2,512,64]{1,2,0:T(8,128)S(1)}, s32[2]{0:T(128)S(1)}, f32[1024,2,32]{0,2,1:T(8,128)S(1)}, f32[1024,2,32]{0,2,1:T(8,128)S(1)}, /*...) while((s32[]{:T(128)}, f32[2,512,64]{1,2,0:T(8,128)S(1)}, ...), condition=%wide.region_8.8_spmd, body=%wide.region_5.7_spmd.sunk | while | flops 811595776 | bytes 17847476 | solution.py:88
  185.7 25.5 %while.33 = (s32[]{:T(128)}, f32[2,512,64]{1,2,0:T(8,128)S(1)}, s32[2]{0:T(128)S(1)}, f32[1024,2,32]{0,2,1:T(8,128)S(1)}, f32[1024,2,32]{0,2,1:T(8,128)S(1)}, /*...) while((s32[]{:T(128)}, f32[2,512,64]{1,2,0:T(8,128)S(1)}, ...), condition=%wide.region_8.8_spmd, body=%wide.region_5.7_spmd.sunk | while | flops 811595776 | bytes 17847476 | solution.py:88
  213.5 25.5 %while.33 = (s32[]{:T(128)}, f32[2,512,64]{1,2,0:T(8,128)S(1)}, s32[2]{0:T(128)S(1)}, f32[1024,2,32]{0,2,1:T(8,128)S(1)}, f32[1024,2,32]{0,2,1:T(8,128)S(1)}, /*...) while((s32[]{:T(128)}, f32[2,512,64]{1,2,0:T(8,128)S(1)}, ...), condition=%wide.region_8.8_spmd, body=%wide.region_5.7_spmd.sunk | while | flops 811595776 | bytes 17847476 | solution.py:88
  241.3 25.5 %while.33 = (s32[]{:T(128)}, f32[2,512,64]{1,2,0:T(8,128)S(1)}, s32[2]{0:T(128)S(1)}, f32[1024,2,32]{0,2,1:T(8,128)S(1)}, f32[1024,2,32]{0,2,1:T(8,128)S(1)}, /*...) while((s32[]{:T(128)}, f32[2,512,64]{1,2,0:T(8,128)S(1)}, ...), condition=%wide.region_8.8_spmd, body=%wide.region_5.7_spmd.sunk | while | flops 811595776 | bytes 17847476 | solution.py:88
  350.4 393.9 %while.32 = (s32[]{:T(128)}, f32[8,16,256,128]{3,2,1,0:T(8,128)}, s32[8]{0:T(128)S(1)}, f32[32,32,128]{0,2,1:T(8,128)}, f32[32,32,256]{2,0,1:T(8,128)S(1)}, /*in...) while((s32[]{:T(128)}, f32[8,16,256,128]{3,2,1,0:T(8,128)}, ...), condition=%wide.region_13.14_spmd, body=%wide.region_12.13_spmd.sunk | while | flops 8057257984 | bytes 37486768 | solution.py:122
  351.7 14.4 %convolution_multiply_fusion.3 = f32[32,16,32,256]{3,1,2,0:T(8,128)S(1)} fusion(f32[32,32,256]{2,0,1:T(8,128)S(1)} %get-tuple-element.424, f32[32,32,128]{0,2,1:T(8,128)} %get-tuple-element.423, s32[]{:T(128)S(6)} %select_n.9), kind=kOutput, calls=%fused_computation.16.clone.1 | convolution fusion | flops 1614807040 | bytes 18087940 | tf_op jit(solution)/shard_map/while/body/eval_jaxpr/sci,sdj->ijcd/dot_general | solution.py:116
  366.1 32.8 %bitcast_dynamic-update-slice_fusion.4 = f32[8,16,256,128]{3,2,1,0:T(8,128)} fusion(f32[8,16,256,128]{3,2,1,0:T(8,128)} %get-tuple-element.411, s32[]{:T(128)S(6)} %copy.191, f32[16,256,1024]{1,0,2:T(8,128)S(1)} %bitcast.139, f32[1024,128]{1,0:T(8,128)S(1)} %get-tuple-element.425), kind=kOutput, calls=%fused_computation.17.clone.1 | convolution fusion | flops 6442450944 | bytes 19398660 | tf_op jit(solution)/shard_map/while/body/eval_jaxpr/dot_general | solution.py:18
  400.1 14.4 %convolution_multiply_fusion.3 = f32[32,16,32,256]{3,1,2,0:T(8,128)S(1)} fusion(f32[32,32,256]{2,0,1:T(8,128)S(1)} %get-tuple-element.424, f32[32,32,128]{0,2,1:T(8,128)} %get-tuple-element.423, s32[]{:T(128)S(6)} %select_n.9), kind=kOutput, calls=%fused_computation.16.clone.1 | convolution fusion | flops 1614807040 | bytes 18087940 | tf_op jit(solution)/shard_map/while/body/eval_jaxpr/sci,sdj->ijcd/dot_general | solution.py:116
  414.5 32.8 %bitcast_dynamic-update-slice_fusion.4 = f32[8,16,256,128]{3,2,1,0:T(8,128)} fusion(f32[8,16,256,128]{3,2,1,0:T(8,128)} %get-tuple-element.411, s32[]{:T(128)S(6)} %copy.191, f32[16,256,1024]{1,0,2:T(8,128)S(1)} %bitcast.139, f32[1024,128]{1,0:T(8,128)S(1)} %get-tuple-element.425), kind=kOutput, calls=%fused_computation.17.clone.1 | convolution fusion | flops 6442450944 | bytes 19398660 | tf_op jit(solution)/shard_map/while/body/eval_jaxpr/dot_general | solution.py:18
  448.4 14.4 %convolution_multiply_fusion.3 = f32[32,16,32,256]{3,1,2,0:T(8,128)S(1)} fusion(f32[32,32,256]{2,0,1:T(8,128)S(1)} %get-tuple-element.424, f32[32,32,128]{0,2,1:T(8,128)} %get-tuple-element.423, s32[]{:T(128)S(6)} %select_n.9), kind=kOutput, calls=%fused_computation.16.clone.1 | convolution fusion | flops 1614807040 | bytes 18087940 | tf_op jit(solution)/shard_map/while/body/eval_jaxpr/sci,sdj->ijcd/dot_general | solution.py:116
  462.8 32.8 %bitcast_dynamic-update-slice_fusion.4 = f32[8,16,256,128]{3,2,1,0:T(8,128)} fusion(f32[8,16,256,128]{3,2,1,0:T(8,128)} %get-tuple-element.411, s32[]{:T(128)S(6)} %copy.191, f32[16,256,1024]{1,0,2:T(8,128)S(1)} %bitcast.139, f32[1024,128]{1,0:T(8,128)S(1)} %get-tuple-element.425), kind=kOutput, calls=%fused_computation.17.clone.1 | convolution fusion | flops 6442450944 | bytes 19398660 | tf_op jit(solution)/shard_map/while/body/eval_jaxpr/dot_general | solution.py:18
  511.2 32.8 %bitcast_dynamic-update-slice_fusion.4 = f32[8,16,256,128]{3,2,1,0:T(8,128)} fusion(f32[8,16,256,128]{3,2,1,0:T(8,128)} %get-tuple-element.411, s32[]{:T(128)S(6)} %copy.191, f32[16,256,1024]{1,0,2:T(8,128)S(1)} %bitcast.139, f32[1024,128]{1,0:T(8,128)S(1)} %get-tuple-element.425), kind=kOutput, calls=%fused_computation.17.clone.1 | convolution fusion | flops 6442450944 | bytes 19398660 | tf_op jit(solution)/shard_map/while/body/eval_jaxpr/dot_general | solution.py:18
  559.5 32.8 %bitcast_dynamic-update-slice_fusion.4 = f32[8,16,256,128]{3,2,1,0:T(8,128)} fusion(f32[8,16,256,128]{3,2,1,0:T(8,128)} %get-tuple-element.411, s32[]{:T(128)S(6)} %copy.191, f32[16,256,1024]{1,0,2:T(8,128)S(1)} %bitcast.139, f32[1024,128]{1,0:T(8,128)S(1)} %get-tuple-element.425), kind=kOutput, calls=%fused_computation.17.clone.1 | convolution fusion | flops 6442450944 | bytes 19398660 | tf_op jit(solution)/shard_map/while/body/eval_jaxpr/dot_general | solution.py:18
  593.5 14.4 %convolution_multiply_fusion.3 = f32[32,16,32,256]{3,1,2,0:T(8,128)S(1)} fusion(f32[32,32,256]{2,0,1:T(8,128)S(1)} %get-tuple-element.424, f32[32,32,128]{0,2,1:T(8,128)} %get-tuple-element.423, s32[]{:T(128)S(6)} %select_n.9), kind=kOutput, calls=%fused_computation.16.clone.1 | convolution fusion | flops 1614807040 | bytes 18087940 | tf_op jit(solution)/shard_map/while/body/eval_jaxpr/sci,sdj->ijcd/dot_general | solution.py:116
  607.9 32.8 %bitcast_dynamic-update-slice_fusion.4 = f32[8,16,256,128]{3,2,1,0:T(8,128)} fusion(f32[8,16,256,128]{3,2,1,0:T(8,128)} %get-tuple-element.411, s32[]{:T(128)S(6)} %copy.191, f32[16,256,1024]{1,0,2:T(8,128)S(1)} %bitcast.139, f32[1024,128]{1,0:T(8,128)S(1)} %get-tuple-element.425), kind=kOutput, calls=%fused_computation.17.clone.1 | convolution fusion | flops 6442450944 | bytes 19398660 | tf_op jit(solution)/shard_map/while/body/eval_jaxpr/dot_general | solution.py:18
  641.9 14.4 %convolution_multiply_fusion.3 = f32[32,16,32,256]{3,1,2,0:T(8,128)S(1)} fusion(f32[32,32,256]{2,0,1:T(8,128)S(1)} %get-tuple-element.424, f32[32,32,128]{0,2,1:T(8,128)} %get-tuple-element.423, s32[]{:T(128)S(6)} %select_n.9), kind=kOutput, calls=%fused_computation.16.clone.1 | convolution fusion | flops 1614807040 | bytes 18087940 | tf_op jit(solution)/shard_map/while/body/eval_jaxpr/sci,sdj->ijcd/dot_general | solution.py:116
  656.3 32.8 %bitcast_dynamic-update-slice_fusion.4 = f32[8,16,256,128]{3,2,1,0:T(8,128)} fusion(f32[8,16,256,128]{3,2,1,0:T(8,128)} %get-tuple-element.411, s32[]{:T(128)S(6)} %copy.191, f32[16,256,1024]{1,0,2:T(8,128)S(1)} %bitcast.139, f32[1024,128]{1,0:T(8,128)S(1)} %get-tuple-element.425), kind=kOutput, calls=%fused_computation.17.clone.1 | convolution fusion | flops 6442450944 | bytes 19398660 | tf_op jit(solution)/shard_map/while/body/eval_jaxpr/dot_general | solution.py:18
  690.2 14.4 %convolution_multiply_fusion.3 = f32[32,16,32,256]{3,1,2,0:T(8,128)S(1)} fusion(f32[32,32,256]{2,0,1:T(8,128)S(1)} %get-tuple-element.424, f32[32,32,128]{0,2,1:T(8,128)} %get-tuple-element.423, s32[]{:T(128)S(6)} %select_n.9), kind=kOutput, calls=%fused_computation.16.clone.1 | convolution fusion | flops 1614807040 | bytes 18087940 | tf_op jit(solution)/shard_map/while/body/eval_jaxpr/sci,sdj->ijcd/dot_general | solution.py:116
  704.6 32.8 %bitcast_dynamic-update-slice_fusion.4 = f32[8,16,256,128]{3,2,1,0:T(8,128)} fusion(f32[8,16,256,128]{3,2,1,0:T(8,128)} %get-tuple-element.411, s32[]{:T(128)S(6)} %copy.191, f32[16,256,1024]{1,0,2:T(8,128)S(1)} %bitcast.139, f32[1024,128]{1,0:T(8,128)S(1)} %get-tuple-element.425), kind=kOutput, calls=%fused_computation.17.clone.1 | convolution fusion | flops 6442450944 | bytes 19398660 | tf_op jit(solution)/shard_map/while/body/eval_jaxpr/dot_general | solution.py:18
  770.0 57.5 %fusion.21 = f32[128,256,512]{2,1,0:T(8,128)} fusion(f32[128,256,128]{2,1,0:T(8,128)S(1)} %bitcast_add_fusion, f32[128,256]{1,0:T(8,128)S(1)} %add_rsqrt_fusion, f32[128,256]{1,0:T(8,128)S(1)} %broadcast_multiply_fusion, f32[128]{0:T(128)S(1)} %copy-done.9, f32[128,512]{1,0:T(8,128)S(1)} %copy-done), kind=kOutput, calls=%fused_computation.29 | convolution fusion | flops 25782386688 | bytes 84410880 | tf_op jit(solution)/shard_map/dot_general | solution.py:18
  827.5 59.1 %add_add_fusion = f32[128,256,128]{2,1,0:T(8,128)} fusion(f32[128,256,128]{2,1,0:T(8,128)S(1)} %bitcast_add_fusion, f32[128,256,512]{2,1,0:T(8,128)} %fusion.21, f32[512]{0:T(512)S(1)} %copy-done.10, f32[128]{0:T(128)S(1)} %copy-done.9, f32[512,128]{1,0:T(8,128)S(1)} %copy-done.5), kind=kOutput, calls=%fused_computation.38 | convolution fusion | flops 25811746816 | bytes 100928000 | tf_op jit(solution)/shard_map/dot_general | solution.py:18
  (181 shorter events, 349.5 us)
Async XLA Ops:
  7.2 762.8 %copy-start = (f32[128,512]{1,0:T(8,128)S(1)}, f32[128,512]{1,0:T(8,128)}, u32[]{:S(2)}) copy-start(f32[128,512]{1,0:T(8,128)} %param.37) | copy-start | bytes 786436
  7.2 19.6 %copy-start.11 = (f32[128,8]{0,1:T(8,128)S(1)}, f32[128,8]{0,1:T(8,128)}, u32[]{:S(2)}) copy-start(f32[128,8]{0,1:T(8,128)} %param.30) | copy-start | bytes 12292
  7.2 149.6 %all-gather.3.cloned.1.call-start = ((), (), s32[]{:S(2)}) async-start(), calls=%async_computation.7 | async-start | bytes 9437184 | tf_op jit(solution)/shard_map/all_gather | solution.py:54
  15.5 11.3 %copy-start.1 = (f32[128,256,128]{2,1,0:T(8,128)S(1)}, f32[128,256,128]{2,1,0:T(8,128)}, u32[]{:S(2)}) copy-start(f32[128,256,128]{2,1,0:T(8,128)} %param.24) | copy-start | bytes 50331652
  26.8 48.1 %copy-start.2 = (f32[4,256,256]{2,1,0:T(8,128)S(1)}, f32[4,256,256]{2,1,0:T(8,128)}, u32[]{:S(2)}) copy-start(f32[4,256,256]{2,1,0:T(8,128)} %param.23) | copy-start | bytes 3145732
  26.8 48.7 %copy-start.6 = (f32[256,256]{1,0:T(8,128)S(1)}, f32[256,256]{1,0:T(8,128)}, u32[]{:S(2)}) copy-start(f32[256,256]{1,0:T(8,128)} %param.28) | copy-start | bytes 786436
  26.8 48.7 %copy-start.13 = (f32[256]{0:T(256)S(1)}, f32[256]{0:T(256)}, u32[]{:S(2)}) copy-start(f32[256]{0:T(256)} %param.29) | copy-start | bytes 3076
  77.8 15.9 %all-to-all-start.4 = ((f32[4,256,256]{1,0,2:T(4,128)}), f32[4,256,256]{1,0,2:T(4,128)S(1)}, u32[]{:S(2)}, u32[]{:S(2)}) async-start(f32[4,256,256]{1,0,2:T(4,128)} %copy.114), calls=%async_computation.4 | async-start | bytes 2097152 | tf_op jit(solution)/shard_map/all_to_all | solution.py:59
  93.8 16.7 %all-to-all-start.2 = ((f32[4,256,256]{1,0,2:T(4,128)}), f32[4,256,256]{1,0,2:T(4,128)S(1)}, u32[]{:S(2)}, u32[]{:S(2)}) async-start(f32[4,256,256]{1,0,2:T(4,128)} %copy.109), calls=%async_computation.2 | async-start | bytes 2097152 | tf_op jit(solution)/shard_map/all_to_all | solution.py:58
  110.5 17.6 %all-to-all-start.1 = ((f32[4,256,256]{1,0,2:T(4,128)}), f32[4,256,256]{1,0,2:T(4,128)}, u32[]{:S(2)}, u32[]{:S(2)}) async-start(f32[4,256,256]{1,0,2:T(4,128)} %copy.106), calls=%async_computation.1 | async-start | bytes 2097152 | tf_op jit(solution)/shard_map/all_to_all | solution.py:57
  128.1 17.1 %all-to-all-start = ((f32[4,256,256]{1,0,2:T(4,128)}), f32[4,256,256]{1,0,2:T(4,128)S(1)}, u32[]{:S(2)}, u32[]{:S(2)}) async-start(f32[4,256,256]{1,0,2:T(4,128)} %copy.103), calls=%async_computation | async-start | bytes 2097152 | tf_op jit(solution)/shard_map/all_to_all | solution.py:56
  156.8 122.6 %copy-start.3 = (f32[4,256,256]{2,1,0:T(8,128)S(1)}, f32[4,256,256]{2,1,0:T(8,128)}, u32[]{:S(2)}) copy-start(f32[4,256,256]{2,1,0:T(8,128)} %param.23) | copy-start | bytes 3145732
  268.0 34.8 %copy-start.12 = (f32[256]{0:T(256)S(1)}, f32[256]{0:T(256)}, u32[]{:S(2)}) copy-start(f32[256]{0:T(256)} %param.32) | copy-start | bytes 3076
  268.0 37.7 %copy-start.7 = (f32[256,32]{0,1:T(8,128)S(1)}, f32[256,32]{0,1:T(8,128)}, u32[]{:S(2)}) copy-start(f32[256,32]{0,1:T(8,128)} %param.34) | copy-start | bytes 98308
  268.0 39.2 %copy-start.8 = (f32[256,32]{0,1:T(8,128)S(1)}, f32[256,32]{0,1:T(8,128)}, u32[]{:S(2)}) copy-start(f32[256,32]{0,1:T(8,128)} %param.33) | copy-start | bytes 98308
  275.5 17.8 %all-to-all-start.5 = ((f32[4,1,65536]{2,1,0:T(1,128)}), f32[4,1,65536]{2,1,0:T(1,128)S(1)}, u32[]{:S(2)}, u32[]{:S(2)}) async-start(f32[4,1,65536]{2,1,0:T(1,128)} %reshape.117), calls=%async_computation.5 | async-start | bytes 2097152 | tf_op jit(solution)/shard_map/all_to_all | solution.py:93
  279.1 69.4 %all-gather.5.cloned.1.call-start = ((), (), s32[]{:S(2)}) async-start(), calls=%async_computation.8 | async-start | bytes 1179648 | tf_op jit(solution)/shard_map/all_gather | solution.py:110
  298.5 51.9 %copy-start.4 = (f32[1024,128]{1,0:T(8,128)S(1)}, f32[1024,128]{1,0:T(8,128)}, u32[]{:S(2)}) copy-start(f32[1024,128]{1,0:T(8,128)} %param.35) | copy-start | bytes 1572868
  323.7 19.1 %all-to-all-start.6 = ((f32[8,1,16384]{2,1,0:T(1,128)}), f32[8,1,16384]{2,1,0:T(1,128)S(1)}, u32[]{:S(2)}, u32[]{:S(2)}) async-start(f32[8,1,16384]{2,1,0:T(1,128)} %reshape.119), calls=%async_computation.6 | async-start | bytes 1048576 | tf_op jit(solution)/shard_map/all_to_all | solution.py:105
  744.3 11.4 %copy-start.9 = (f32[128]{0:T(128)S(1)}, f32[128]{0:T(128)}, u32[]{:S(2)}) copy-start(f32[128]{0:T(128)} %param.36) | copy-start | bytes 1540
  769.9 57.5 %copy-start.5 = (f32[512,128]{1,0:T(8,128)S(1)}, f32[512,128]{1,0:T(8,128)}, u32[]{:S(2)}) copy-start(f32[512,128]{1,0:T(8,128)} %param.39) | copy-start | bytes 786436
  769.9 57.5 %copy-start.10 = (f32[512]{0:T(512)S(1)}, f32[512]{0:T(512)}, u32[]{:S(2)}) copy-start(f32[512]{0:T(512)} %param.38) | copy-start | bytes 6148
Sparse Core Ops, SparseCore 0:
  75.0 81.7 all-gather.2
  307.3 19.8 all-gather.4
where the time goes:
time: 902 us; the launch traced here: 894 us
  matrix products  618 us (69%)
  waiting for transfers between devices  70 us (8%)
  other arithmetic  64.1 us (7%)
  local copies, waits for them, and re-layouts  56.5 us (6%)
  blocking collectives  29.6 us (3%)
  starting transfers between devices  23.1 us (3%)
  loops' own time  17.1 us (2%)
  between operations  14.7 us (2%)
    dot_general x15, matrix products, matrix_multiply(): jnp.dot(first_arr, second_arr, precision=finest_precision, preferred_elem...  391 us
    dot_general x8, matrix products, outer_block(): jnp.einsum('sci,sdj->ijcd', left_part, right_all, precision=finest_precis...  115 us
    dot_general x8, matrix products, per_block(): jnp.einsum('qhd,khd->hqk', query_rows, key_item, precision=finest_precision)  45.8 us
    dot_general x8, matrix products, per_block(): jnp.einsum('hqk,khd->qhd', softmax_probabilities, value_item, precision=f...  36.8 us
    dot_general x1, matrix products, per_device(): jnp.einsum('ijc,ch->hij', layer_normalize(pair_state), pair_bias_weight,...  27.4 us
    reduce_sum x4, other arithmetic, layer_normalize(): variance = jnp.mean(centered * centered, axis=-1, keepdims=True)  21.3 us
    all_to_all x1, blocking collectives, per_device(): lax.all_to_all(bias_tile, 'narrow', split_axis=0, concat_axis=2, tiled=True)  19.1 us
  transfers between devices with their start and end apart: 8, of which 7 were waited for; matrix products, arithmetic and copies ran while one was open for 4% of the time, Pallas kernels for 0%

commit v1 on v0

--- a/solution.py
+++ b/solution.py
@@ -102,7 +102,12 @@
         "srm,mc->scr", outer_product_normed, second_factor_projector, precision=finest_precision
     )
     left_rows = lax.all_gather(left_proj, "narrow", axis=2, tiled=True)
-    left_all = lax.all_to_all(left_rows, "wide", split_axis=2, concat_axis=0, tiled=True)
+    left_all = jnp.concatenate(
+        lax.all_to_all(
+            jnp.stack(jnp.split(left_rows, lax.axis_size("wide"), axis=2)), "wide", 0, 0
+        ),
+        axis=0,
+    )
     seq_count = left_all.shape[0]
     tile_rows = left_all.shape[2]
     tile_cols = right_proj.shape[2]

time: 902 us -> 918 us (1.018)
  loops' own time: 17.1 us -> 37.6 us
    another operation x1, loops' own time: 11.5 us -> 32 us  [per_device(): lax.map(outer_block, jnp.arange(tile_rows // block_rows, dtype=jnp.int32))]
where the time goes in v1:
time: 918 us; the launch traced here: 910 us
  matrix products  618 us (67%)
  waiting for transfers between devices  70 us (8%)
  other arithmetic  60.4 us (7%)
  local copies, waits for them, and re-layouts  56.8 us (6%)
  loops' own time  37.6 us (4%)
  blocking collectives  29.6 us (3%)
  starting transfers between devices  22.7 us (2%)
  between operations  14.7 us (2%)
    dot_general x15, matrix products, matrix_multiply(): jnp.dot(first_arr, second_arr, precision=finest_precision, preferred_elem...  391 us
    dot_general x8, matrix products, outer_block(): jnp.einsum('sci,sdj->ijcd', left_part, right_all, precision=finest_precis...  115 us
    dot_general x8, matrix products, per_block(): jnp.einsum('qhd,khd->hqk', query_rows, key_item, precision=finest_precision)  45.8 us
    dot_general x8, matrix products, per_block(): jnp.einsum('hqk,khd->qhd', softmax_probabilities, value_item, precision=f...  36.8 us
    another operation x1, loops' own time, per_device(): lax.map(outer_block, jnp.arange(tile_rows // block_rows, dtype=jnp.int32))  32 us
    dot_general x1, matrix products, per_device(): jnp.einsum('ijc,ch->hij', layer_normalize(pair_state), pair_bias_weight,...  27.4 us
    reduce_sum x4, other arithmetic, layer_normalize(): variance = jnp.mean(centered * centered, axis=-1, keepdims=True)  21.3 us
    all_to_all x1, blocking collectives, per_device(): lax.all_to_all(bias_tile, 'narrow', split_axis=0, concat_axis=2, tiled=True)  19.1 us
  transfers between devices with their start and end apart: 8, of which 7 were waited for; matrix products, arithmetic and copies ran while one was open for 4% of the time, Pallas kernels for 0%

profile of v1, /device:TPU:0, one launch (start us, length us, event | category | flops | bytes accessed | tf_op | source)
XLA Modules:
  0.0 909.9 jit_solution(7289599455200662099)
XLA Ops:
  26.8 27.4 %fusion.36 = f32[8,128,256]{2,0,1:T(8,128)S(1)} fusion(f32[128,256,128]{2,1,0:T(8,128)S(1)} %copy-done.1, f32[128,256]{1,0:T(8,128)S(1)} %add_rsqrt_fusion.1, f32[128,256]{1,0:T(8,128)S(1)} %broadcast_multiply_fusion.1, f32[128,8]{0,1:T(8,128)S(1)} %copy-done.12), kind=kOutput, calls=%fused_computation.49 | convolution fusion | flops 411041792 | bytes 18092032 | tf_op jit(solution)/shard_map/ijc,ch->hij/dot_general | solution.py:50
  54.6 19.1 %all_to_all.104 = f32[8,128,256]{2,1,0:T(8,128)S(1)} all-to-all(f32[8,128,256]{2,1,0:T(8,128)S(1)} %copy.81), channel_id=1, replica_groups=mesh['wide'=8,'narrow'=4] {'narrow'}, dimensions={0} | all-to-all | bytes 2097152 | tf_op jit(solution)/shard_map/all_to_all | solution.py:53
  156.8 110.9 %while.31 = (s32[]{:T(128)}, f32[4,1024,64]{1,2,0:T(8,128)}, f32[4,1024,64]{1,2,0:T(8,128)S(1)}, f32[4,1024,64]{1,2,0:T(8,128)}, f32[4,1024,64]{1,2,0:T(8,128)},...) while((s32[]{:T(128)}, f32[4,1024,64]{1,2,0:T(8,128)}, ...), condition=%wide.region_9.10_spmd, body=%wide.region_4.9_spmd.sunk | while | flops 811595776 | bytes 20993444 | solution.py:91
  158.0 25.5 %while.33 = (s32[]{:T(128)}, f32[2,512,64]{1,2,0:T(8,128)S(1)}, s32[2]{0:T(128)S(1)}, f32[1024,2,32]{0,2,1:T(8,128)S(1)}, f32[1024,2,32]{0,2,1:T(8,128)S(1)}, /*...) while((s32[]{:T(128)}, f32[2,512,64]{1,2,0:T(8,128)S(1)}, ...), condition=%wide.region_8.8_spmd, body=%wide.region_5.7_spmd.sunk | while | flops 811595776 | bytes 17847476 | solution.py:88
  185.7 25.5 %while.33 = (s32[]{:T(128)}, f32[2,512,64]{1,2,0:T(8,128)S(1)}, s32[2]{0:T(128)S(1)}, f32[1024,2,32]{0,2,1:T(8,128)S(1)}, f32[1024,2,32]{0,2,1:T(8,128)S(1)}, /*...) while((s32[]{:T(128)}, f32[2,512,64]{1,2,0:T(8,128)S(1)}, ...), condition=%wide.region_8.8_spmd, body=%wide.region_5.7_spmd.sunk | while | flops 811595776 | bytes 17847476 | solution.py:88
  213.4 25.5 %while.33 = (s32[]{:T(128)}, f32[2,512,64]{1,2,0:T(8,128)S(1)}, s32[2]{0:T(128)S(1)}, f32[1024,2,32]{0,2,1:T(8,128)S(1)}, f32[1024,2,32]{0,2,1:T(8,128)S(1)}, /*...) while((s32[]{:T(128)}, f32[2,512,64]{1,2,0:T(8,128)S(1)}, ...), condition=%wide.region_8.8_spmd, body=%wide.region_5.7_spmd.sunk | while | flops 811595776 | bytes 17847476 | solution.py:88
  241.1 25.5 %while.33 = (s32[]{:T(128)}, f32[2,512,64]{1,2,0:T(8,128)S(1)}, s32[2]{0:T(128)S(1)}, f32[1024,2,32]{0,2,1:T(8,128)S(1)}, f32[1024,2,32]{0,2,1:T(8,128)S(1)}, /*...) while((s32[]{:T(128)}, f32[2,512,64]{1,2,0:T(8,128)S(1)}, ...), condition=%wide.region_8.8_spmd, body=%wide.region_5.7_spmd.sunk | while | flops 811595776 | bytes 17847476 | solution.py:88
  345.4 415.1 %while.32 = (s32[]{:T(128)}, f32[8,16,256,128]{3,2,1,0:T(8,128)}, s32[8]{0:T(128)S(1)}, f32[32,32,128]{0,2,1:T(8,128)}, f32[32,32,256]{2,0,1:T(8,128)S(1)}, /*in...) while((s32[]{:T(128)}, f32[8,16,256,128]{3,2,1,0:T(8,128)}, ...), condition=%wide.region_13.14_spmd, body=%wide.region_12.13_spmd.sunk | while | flops 8057257984 | bytes 37486768 | solution.py:127
  366.4 14.4 %convolution_multiply_fusion.3 = f32[32,16,32,256]{3,1,2,0:T(8,128)S(1)} fusion(f32[32,32,256]{2,0,1:T(8,128)S(1)} %get-tuple-element.416, f32[32,32,128]{0,2,1:T(8,128)} %get-tuple-element.415, s32[]{:T(128)S(6)} %select_n.9), kind=kOutput, calls=%fused_computation.16.clone.1 | convolution fusion | flops 1614807040 | bytes 18087940 | tf_op jit(solution)/shard_map/while/body/eval_jaxpr/sci,sdj->ijcd/dot_general | solution.py:121
  380.8 32.8 %bitcast_dynamic-update-slice_fusion.4 = f32[8,16,256,128]{3,2,1,0:T(8,128)} fusion(f32[8,16,256,128]{3,2,1,0:T(8,128)} %get-tuple-element.403, s32[]{:T(128)S(6)} %copy.162, f32[16,256,1024]{1,0,2:T(8,128)S(1)} %bitcast.165, f32[1024,128]{1,0:T(8,128)S(1)} %get-tuple-element.417), kind=kOutput, calls=%fused_computation.17.clone.1 | convolution fusion | flops 6442450944 | bytes 19398660 | tf_op jit(solution)/shard_map/while/body/eval_jaxpr/dot_general | solution.py:18
  415.0 14.4 %convolution_multiply_fusion.3 = f32[32,16,32,256]{3,1,2,0:T(8,128)S(1)} fusion(f32[32,32,256]{2,0,1:T(8,128)S(1)} %get-tuple-element.416, f32[32,32,128]{0,2,1:T(8,128)} %get-tuple-element.415, s32[]{:T(128)S(6)} %select_n.9), kind=kOutput, calls=%fused_computation.16.clone.1 | convolution fusion | flops 1614807040 | bytes 18087940 | tf_op jit(solution)/shard_map/while/body/eval_jaxpr/sci,sdj->ijcd/dot_general | solution.py:121
  429.4 32.8 %bitcast_dynamic-update-slice_fusion.4 = f32[8,16,256,128]{3,2,1,0:T(8,128)} fusion(f32[8,16,256,128]{3,2,1,0:T(8,128)} %get-tuple-element.403, s32[]{:T(128)S(6)} %copy.162, f32[16,256,1024]{1,0,2:T(8,128)S(1)} %bitcast.165, f32[1024,128]{1,0:T(8,128)S(1)} %get-tuple-element.417), kind=kOutput, calls=%fused_computation.17.clone.1 | convolution fusion | flops 6442450944 | bytes 19398660 | tf_op jit(solution)/shard_map/while/body/eval_jaxpr/dot_general | solution.py:18
  478.0 32.8 %bitcast_dynamic-update-slice_fusion.4 = f32[8,16,256,128]{3,2,1,0:T(8,128)} fusion(f32[8,16,256,128]{3,2,1,0:T(8,128)} %get-tuple-element.403, s32[]{:T(128)S(6)} %copy.162, f32[16,256,1024]{1,0,2:T(8,128)S(1)} %bitcast.165, f32[1024,128]{1,0:T(8,128)S(1)} %get-tuple-element.417), kind=kOutput, calls=%fused_computation.17.clone.1 | convolution fusion | flops 6442450944 | bytes 19398660 | tf_op jit(solution)/shard_map/while/body/eval_jaxpr/dot_general | solution.py:18
  512.1 14.4 %convolution_multiply_fusion.3 = f32[32,16,32,256]{3,1,2,0:T(8,128)S(1)} fusion(f32[32,32,256]{2,0,1:T(8,128)S(1)} %get-tuple-element.416, f32[32,32,128]{0,2,1:T(8,128)} %get-tuple-element.415, s32[]{:T(128)S(6)} %select_n.9), kind=kOutput, calls=%fused_computation.16.clone.1 | convolution fusion | flops 1614807040 | bytes 18087940 | tf_op jit(solution)/shard_map/while/body/eval_jaxpr/sci,sdj->ijcd/dot_general | solution.py:121
  526.5 32.8 %bitcast_dynamic-update-slice_fusion.4 = f32[8,16,256,128]{3,2,1,0:T(8,128)} fusion(f32[8,16,256,128]{3,2,1,0:T(8,128)} %get-tuple-element.403, s32[]{:T(128)S(6)} %copy.162, f32[16,256,1024]{1,0,2:T(8,128)S(1)} %bitcast.165, f32[1024,128]{1,0:T(8,128)S(1)} %get-tuple-element.417), kind=kOutput, calls=%fused_computation.17.clone.1 | convolution fusion | flops 6442450944 | bytes 19398660 | tf_op jit(solution)/shard_map/while/body/eval_jaxpr/dot_general | solution.py:18
  560.7 14.4 %convolution_multiply_fusion.3 = f32[32,16,32,256]{3,1,2,0:T(8,128)S(1)} fusion(f32[32,32,256]{2,0,1:T(8,128)S(1)} %get-tuple-element.416, f32[32,32,128]{0,2,1:T(8,128)} %get-tuple-element.415, s32[]{:T(128)S(6)} %select_n.9), kind=kOutput, calls=%fused_computation.16.clone.1 | convolution fusion | flops 1614807040 | bytes 18087940 | tf_op jit(solution)/shard_map/while/body/eval_jaxpr/sci,sdj->ijcd/dot_general | solution.py:121
  575.1 32.8 %bitcast_dynamic-update-slice_fusion.4 = f32[8,16,256,128]{3,2,1,0:T(8,128)} fusion(f32[8,16,256,128]{3,2,1,0:T(8,128)} %get-tuple-element.403, s32[]{:T(128)S(6)} %copy.162, f32[16,256,1024]{1,0,2:T(8,128)S(1)} %bitcast.165, f32[1024,128]{1,0:T(8,128)S(1)} %get-tuple-element.417), kind=kOutput, calls=%fused_computation.17.clone.1 | convolution fusion | flops 6442450944 | bytes 19398660 | tf_op jit(solution)/shard_map/while/body/eval_jaxpr/dot_general | solution.py:18
  609.3 14.4 %convolution_multiply_fusion.3 = f32[32,16,32,256]{3,1,2,0:T(8,128)S(1)} fusion(f32[32,32,256]{2,0,1:T(8,128)S(1)} %get-tuple-element.416, f32[32,32,128]{0,2,1:T(8,128)} %get-tuple-element.415, s32[]{:T(128)S(6)} %select_n.9), kind=kOutput, calls=%fused_computation.16.clone.1 | convolution fusion | flops 1614807040 | bytes 18087940 | tf_op jit(solution)/shard_map/while/body/eval_jaxpr/sci,sdj->ijcd/dot_general | solution.py:121
  623.7 32.8 %bitcast_dynamic-update-slice_fusion.4 = f32[8,16,256,128]{3,2,1,0:T(8,128)} fusion(f32[8,16,256,128]{3,2,1,0:T(8,128)} %get-tuple-element.403, s32[]{:T(128)S(6)} %copy.162, f32[16,256,1024]{1,0,2:T(8,128)S(1)} %bitcast.165, f32[1024,128]{1,0:T(8,128)S(1)} %get-tuple-element.417), kind=kOutput, calls=%fused_computation.17.clone.1 | convolution fusion | flops 6442450944 | bytes 19398660 | tf_op jit(solution)/shard_map/while/body/eval_jaxpr/dot_general | solution.py:18
  672.3 32.8 %bitcast_dynamic-update-slice_fusion.4 = f32[8,16,256,128]{3,2,1,0:T(8,128)} fusion(f32[8,16,256,128]{3,2,1,0:T(8,128)} %get-tuple-element.403, s32[]{:T(128)S(6)} %copy.162, f32[16,256,1024]{1,0,2:T(8,128)S(1)} %bitcast.165, f32[1024,128]{1,0:T(8,128)S(1)} %get-tuple-element.417), kind=kOutput, calls=%fused_computation.17.clone.1 | convolution fusion | flops 6442450944 | bytes 19398660 | tf_op jit(solution)/shard_map/while/body/eval_jaxpr/dot_general | solution.py:18
  706.5 14.4 %convolution_multiply_fusion.3 = f32[32,16,32,256]{3,1,2,0:T(8,128)S(1)} fusion(f32[32,32,256]{2,0,1:T(8,128)S(1)} %get-tuple-element.416, f32[32,32,128]{0,2,1:T(8,128)} %get-tuple-element.415, s32[]{:T(128)S(6)} %select_n.9), kind=kOutput, calls=%fused_computation.16.clone.1 | convolution fusion | flops 1614807040 | bytes 18087940 | tf_op jit(solution)/shard_map/while/body/eval_jaxpr/sci,sdj->ijcd/dot_general | solution.py:121
  720.9 32.8 %bitcast_dynamic-update-slice_fusion.4 = f32[8,16,256,128]{3,2,1,0:T(8,128)} fusion(f32[8,16,256,128]{3,2,1,0:T(8,128)} %get-tuple-element.403, s32[]{:T(128)S(6)} %copy.162, f32[16,256,1024]{1,0,2:T(8,128)S(1)} %bitcast.165, f32[1024,128]{1,0:T(8,128)S(1)} %get-tuple-element.417), kind=kOutput, calls=%fused_computation.17.clone.1 | convolution fusion | flops 6442450944 | bytes 19398660 | tf_op jit(solution)/shard_map/while/body/eval_jaxpr/dot_general | solution.py:18
  786.2 57.5 %fusion.21 = f32[128,256,512]{2,1,0:T(8,128)} fusion(f32[128,256,128]{2,1,0:T(8,128)S(1)} %bitcast_add_fusion, f32[128,256]{1,0:T(8,128)S(1)} %add_rsqrt_fusion, f32[128,256]{1,0:T(8,128)S(1)} %broadcast_multiply_fusion, f32[128]{0:T(128)S(1)} %copy-done.10, f32[128,512]{1,0:T(8,128)S(1)} %copy-done), kind=kOutput, calls=%fused_computation.29 | convolution fusion | flops 25782386688 | bytes 84410880 | tf_op jit(solution)/shard_map/dot_general | solution.py:18
  843.8 59.1 %add_add_fusion = f32[128,256,128]{2,1,0:T(8,128)} fusion(f32[128,256,128]{2,1,0:T(8,128)S(1)} %bitcast_add_fusion, f32[128,256,512]{2,1,0:T(8,128)} %fusion.21, f32[512]{0:T(512)S(1)} %copy-done.11, f32[128]{0:T(128)S(1)} %copy-done.10, f32[512,128]{1,0:T(8,128)S(1)} %copy-done.5), kind=kOutput, calls=%fused_computation.38 | convolution fusion | flops 25811746816 | bytes 100928000 | tf_op jit(solution)/shard_map/dot_general | solution.py:18
  (186 shorter events, 345.3 us)
Async XLA Ops:
  7.2 779.0 %copy-start = (f32[128,512]{1,0:T(8,128)S(1)}, f32[128,512]{1,0:T(8,128)}, u32[]{:S(2)}) copy-start(f32[128,512]{1,0:T(8,128)} %param.37) | copy-start | bytes 786436
  7.2 19.6 %copy-start.12 = (f32[128,8]{0,1:T(8,128)S(1)}, f32[128,8]{0,1:T(8,128)}, u32[]{:S(2)}) copy-start(f32[128,8]{0,1:T(8,128)} %param.30) | copy-start | bytes 12292
  7.2 149.6 %all-gather.3.cloned.1.call-start = ((), (), s32[]{:S(2)}) async-start(), calls=%async_computation.7 | async-start | bytes 9437184 | tf_op jit(solution)/shard_map/all_gather | solution.py:54
  15.5 11.3 %copy-start.1 = (f32[128,256,128]{2,1,0:T(8,128)S(1)}, f32[128,256,128]{2,1,0:T(8,128)}, u32[]{:S(2)}) copy-start(f32[128,256,128]{2,1,0:T(8,128)} %param.24) | copy-start | bytes 50331652
  26.8 48.1 %copy-start.2 = (f32[4,256,256]{2,1,0:T(8,128)S(1)}, f32[4,256,256]{2,1,0:T(8,128)}, u32[]{:S(2)}) copy-start(f32[4,256,256]{2,1,0:T(8,128)} %param.23) | copy-start | bytes 3145732
  26.8 48.7 %copy-start.6 = (f32[256,256]{1,0:T(8,128)S(1)}, f32[256,256]{1,0:T(8,128)}, u32[]{:S(2)}) copy-start(f32[256,256]{1,0:T(8,128)} %param.28) | copy-start | bytes 786436
  26.8 48.7 %copy-start.14 = (f32[256]{0:T(256)S(1)}, f32[256]{0:T(256)}, u32[]{:S(2)}) copy-start(f32[256]{0:T(256)} %param.29) | copy-start | bytes 3076
  77.9 15.9 %all-to-all-start.4 = ((f32[4,256,256]{1,0,2:T(4,128)}), f32[4,256,256]{1,0,2:T(4,128)S(1)}, u32[]{:S(2)}, u32[]{:S(2)}) async-start(f32[4,256,256]{1,0,2:T(4,128)} %copy.83), calls=%async_computation.4 | async-start | bytes 2097152 | tf_op jit(solution)/shard_map/all_to_all | solution.py:59
  93.8 16.7 %all-to-all-start.2 = ((f32[4,256,256]{1,0,2:T(4,128)}), f32[4,256,256]{1,0,2:T(4,128)S(1)}, u32[]{:S(2)}, u32[]{:S(2)}) async-start(f32[4,256,256]{1,0,2:T(4,128)} %copy.78), calls=%async_computation.2 | async-start | bytes 2097152 | tf_op jit(solution)/shard_map/all_to_all | solution.py:58
  110.5 17.6 %all-to-all-start.1 = ((f32[4,256,256]{1,0,2:T(4,128)}), f32[4,256,256]{1,0,2:T(4,128)}, u32[]{:S(2)}, u32[]{:S(2)}) async-start(f32[4,256,256]{1,0,2:T(4,128)} %copy.75), calls=%async_computation.1 | async-start | bytes 2097152 | tf_op jit(solution)/shard_map/all_to_all | solution.py:57
  128.1 17.1 %all-to-all-start = ((f32[4,256,256]{1,0,2:T(4,128)}), f32[4,256,256]{1,0,2:T(4,128)S(1)}, u32[]{:S(2)}, u32[]{:S(2)}) async-start(f32[4,256,256]{1,0,2:T(4,128)} %copy.72), calls=%async_computation | async-start | bytes 2097152 | tf_op jit(solution)/shard_map/all_to_all | solution.py:56
  156.8 122.8 %copy-start.3 = (f32[4,256,256]{2,1,0:T(8,128)S(1)}, f32[4,256,256]{2,1,0:T(8,128)}, u32[]{:S(2)}) copy-start(f32[4,256,256]{2,1,0:T(8,128)} %param.23) | copy-start | bytes 3145732
  267.7 34.7 %copy-start.7 = (f32[256,256]{1,0:T(8,128)S(1)}, f32[256,256]{1,0:T(8,128)}, u32[]{:S(2)}) copy-start(f32[256,256]{1,0:T(8,128)} %param.31) | copy-start | bytes 786436
  267.7 34.7 %copy-start.13 = (f32[256]{0:T(256)S(1)}, f32[256]{0:T(256)}, u32[]{:S(2)}) copy-start(f32[256]{0:T(256)} %param.32) | copy-start | bytes 3076
  267.7 37.3 %copy-start.8 = (f32[256,32]{0,1:T(8,128)S(1)}, f32[256,32]{0,1:T(8,128)}, u32[]{:S(2)}) copy-start(f32[256,32]{0,1:T(8,128)} %param.34) | copy-start | bytes 98308
  267.7 38.7 %copy-start.9 = (f32[256,32]{0,1:T(8,128)S(1)}, f32[256,32]{0,1:T(8,128)}, u32[]{:S(2)}) copy-start(f32[256,32]{0,1:T(8,128)} %param.33) | copy-start | bytes 98308
  271.2 74.3 %copy-start.4 = (f32[1024,128]{1,0:T(8,128)S(1)}, f32[1024,128]{1,0:T(8,128)}, u32[]{:S(2)}) copy-start(f32[1024,128]{1,0:T(8,128)} %param.35) | copy-start | bytes 1572868
  275.7 17.8 %all-to-all-start.5 = ((f32[4,1,65536]{2,1,0:T(1,128)}), f32[4,1,65536]{2,1,0:T(1,128)S(1)}, u32[]{:S(2)}, u32[]{:S(2)}) async-start(f32[4,1,65536]{2,1,0:T(1,128)} %reshape.121), calls=%async_computation.5 | async-start | bytes 2097152 | tf_op jit(solution)/shard_map/all_to_all | solution.py:93
  279.4 64.2 %all-gather.5.cloned.1.call-start = ((), (), s32[]{:S(2)}) async-start(), calls=%async_computation.8 | async-start | bytes 1179648 | tf_op jit(solution)/shard_map/all_gather | solution.py:115
  322.8 18.8 %all-to-all-start.6 = ((f32[8,4,32,128]{3,2,1,0:T(8,128)}), f32[8,4,32,128]{3,2,1,0:T(8,128)S(1)}, u32[]{:S(2)}, u32[]{:S(2)}) async-start(f32[8,4,32,128]{3,2,1,0:T(8,128)} %fusion.67), calls=%async_computation.6 | async-start | bytes 1048576 | tf_op jit(solution)/shard_map/all_to_all | solution.py:106
  760.5 11.4 %copy-start.10 = (f32[128]{0:T(128)S(1)}, f32[128]{0:T(128)}, u32[]{:S(2)}) copy-start(f32[128]{0:T(128)} %param.36) | copy-start | bytes 1540
  786.2 57.5 %copy-start.5 = (f32[512,128]{1,0:T(8,128)S(1)}, f32[512,128]{1,0:T(8,128)}, u32[]{:S(2)}) copy-start(f32[512,128]{1,0:T(8,128)} %param.39) | copy-start | bytes 786436
  786.2 57.5 %copy-start.11 = (f32[512]{0:T(512)S(1)}, f32[512]{0:T(512)}, u32[]{:S(2)}) copy-start(f32[512]{0:T(512)} %param.38) | copy-start | bytes 6148
Sparse Core Ops, SparseCore 0:
  75.0 81.7 all-gather.2
  306.6 19.8 all-gather.4
